TPU v7x, 32 devices: a whole 2x2x4 slice. The times are simulated.
32 devices in a mesh: row: 8 (over z, x), col: 4 (over y, core).
Axes of the slice: x: 2, y: 2, z: 4, core: 2. Of those that a mesh axis runs over, the one named last changes fastest.
Arguments:
- hamiltonian: bfloat16 [2, 2048, 2048], P(None, 'row', 'col'), may hold values from -0.25 to 0.25
- basis_metric: bfloat16 [2048, 2048], P('row', 'col'), may hold values from -0.25 to 0.25
- density: bfloat16 [2, 2048, 2048], P(None, 'row', 'col'), may hold values from -6 to 6
- hamiltonian_keep: int32 [16, 16], P('row', 'col'), may hold values from 0 to 1, as said below
- metric_keep: int32 [16, 16], P('row', 'col'), may hold values from 0 to 1, as said below
- density_keep: int32 [16, 16], P('row', 'col'), may hold values from 0 to 1, as said below
- gradient_keep: int32 [16, 16], P('row', 'col'), may hold values 0 or 1
Outputs:
- gradient: float32 [2, 2048, 2048], P(None, 'row', 'col')
Inputs may be any that keep to these rules, and one draw needn't show every extreme that they name: `hamiltonian_keep`: each block row has at most 4 blocks in the pattern, and some rows have exactly 4. `metric_keep`: each block row has at most 4 blocks in the pattern, and some rows have exactly 4. `density_keep`: each block row keeps at most 7 blocks, and some rows keep exactly 7.
All inputs are finite; a program needn't handle non-finite values. No bound on the sum of `gradient_keep` on one device may be relied on, other than what follows from the above.
Results may differ from a plain program's by a relative error of at most 0.0029.
Values may be sent and summed in bfloat16 or wider, within the bound.
No kernel may reach another device: no remote copies, remote signals or barrier semaphores. Data moves between devices by JAX's collectives and lax.ppermute only.
A program may use at most 64 MiB of HBM per device.

v0:
```python
import jax
import jax.numpy as jnp
from jax import lax
from jax.sharding import PartitionSpec as P

BLOCK = 128


def widen(keep):
    return jnp.repeat(jnp.repeat(keep, BLOCK, axis=0), BLOCK, axis=1) > 0


def first_terms(rows_part, cols_part):
    hterm = jnp.einsum("srl,slc->src", rows_part[:2], cols_part, preferred_element_type=jnp.float32)
    sterm = jnp.einsum("rl,slc->src", rows_part[2], cols_part, preferred_element_type=jnp.float32)
    return jnp.concatenate([hterm, sterm], axis=0)


def second_terms(rows_part, cols_part):
    left = jnp.einsum(
        "srl,lc->src", rows_part[:2], cols_part[2], preferred_element_type=jnp.float32
    )
    right = jnp.einsum(
        "srl,slc->src", rows_part[2:], cols_part[:2], preferred_element_type=jnp.float32
    )
    return left - right


def body(
    hamiltonian, basis_metric, density, hamiltonian_keep, metric_keep, density_keep, gradient_keep
):
    kohn_sham = jnp.where(widen(hamiltonian_keep)[None], hamiltonian, jnp.zeros_like(hamiltonian))
    smat = jnp.where(widen(metric_keep), basis_metric, jnp.zeros_like(basis_metric))
    filtered = jnp.where(widen(density_keep)[None], density, jnp.zeros_like(density))
    operators = jnp.concatenate([kohn_sham, smat[None]], axis=0)
    density_cols = lax.all_gather(filtered, "row", axis=1, tiled=True)
    cols_part = density_cols
    products = first_terms(lax.all_gather(operators, "col", axis=2, tiled=True), cols_part)
    products = products.astype(jnp.bfloat16)
    operator_cols = lax.all_gather(operators, "row", axis=1, tiled=True)
    cols_part = operator_cols
    commut = second_terms(lax.all_gather(products, "col", axis=2, tiled=True), cols_part)
    grad_mask = widen(gradient_keep)[None]
    return jnp.where(grad_mask, commut, jnp.zeros_like(commut))


def solution(mesh):
    in_specs = (
        P(None, "row", "col"),
        P("row", "col"),
        P(None, "row", "col"),
        P("row", "col"),
        P("row", "col"),
        P("row", "col"),
        P("row", "col"),
    )
    out_specs = P(None, "row", "col")
    return jax.shard_map(body, mesh=mesh, in_specs=in_specs, out_specs=out_specs, check_vma=False)
```

profile of v0, /device:TPU:0, one launch (start us, length us, event | category | flops | bytes accessed | tf_op | source)
XLA Modules:
  0.0 267.1 jit_solution(11964594302407016854)
XLA Ops:
  6.5 0.0 copy-start.4
  6.5 0.0 copy-start
  6.5 0.0 all-gather.5.cloned.1.call-start
  6.5 0.7 broadcast_compare_fusion.2
  7.3 0.3 broadcast_in_dim.61
  7.6 0.1 copy.23
  7.7 0.7 broadcast_compare_fusion.1
  8.4 1.1 broadcast_select_fusion.1
  9.5 0.3 broadcast_in_dim.64
  9.9 1.0 fusion.6
  10.9 1.0 pad_maximum_fusion.1
  11.9 0.0 all-gather.5.cloned.1.call-update
  11.9 0.0 all-gather.7.cloned.1.call-start
  11.9 0.0 copy-done.4
  12.0 0.3 broadcast_in_dim.68
  12.3 0.1 copy.22
  12.4 0.0 copy-done
  12.4 0.9 broadcast_select_fusion
  13.2 0.0 all-gather.7.cloned.1.call-update
  13.3 0.0 all-gather.11.cloned.1.call-start
  13.3 0.7 all-gather.11.cloned.1.call-update
  14.0 0.0 all-gather.9.cloned.1.call-start
  14.1 29.2 %all-gather.5.cloned.1.call-done = bf16[3,256,2048]{2,1,0:T(8,128)(2,1)} async-done(((bf16[3,256,512]{2,1,0:T(8,128)(2,1)}), bf16[3,256,2048]{2,1,0:T(8,128)(2,1)}) %all-gather.5.cloned.1.call-update) | async-done | bytes 3145744 | tf_op jit(solution)/shard_map/all_gather | solution.py:38
  43.3 0.0 copy-start.3
  43.3 75.6 %all-gather.7.cloned.1.call-done = bf16[2,2048,512]{2,1,0:T(8,128)(2,1)} async-done(((bf16[2,256,512]{2,1,0:T(8,128)(2,1)}), bf16[2,2048,512]{2,1,0:T(8,128)(2,1)}) %all-gather.7.cloned.1.call-update) | async-done | bytes 4194320 | tf_op jit(solution)/shard_map/all_gather | solution.py:36
  118.9 0.0 copy-start.1
  118.9 3.9 %fusion.5 = bf16[2,256,512]{2,1,0:T(8,128)(2,1)S(1)} fusion(bf16[2,2048,512]{2,1,0:T(8,128)(2,1)} %all-gather.7.cloned.1.call-done, bf16[3,256,2048]{2,1,0:T(8,128)(2,1)} %all-gather.5.cloned.1.call-done), kind=kOutput, calls=%fused_computation.8 | convolution fusion | flops 1074003968 | bytes 5767168 | tf_op jit(solution)/shard_map/rl,slc->src/dot_general | solution.py:15
  122.8 0.0 copy-done.3
  122.8 0.0 copy-done.1
  122.8 0.0 copy-start.5
  122.8 1.3 convolution_convert_fusion
  124.1 1.1 pad_maximum_fusion
  125.2 0.0 all-gather.9.cloned.1.call-update
  125.2 0.0 copy-done.5
  125.2 0.3 broadcast_in_dim.58
  125.6 0.1 copy.24
  125.6 92.7 %all-gather.11.cloned.1.call-done = bf16[3,2048,512]{2,1,0:T(8,128)(2,1)} async-done(((bf16[3,256,512]{2,1,0:T(8,128)(2,1)}), bf16[3,2048,512]{2,1,0:T(8,128)(2,1)}) %all-gather.11.cloned.1.call-update) | async-done | bytes 6291472 | tf_op jit(solution)/shard_map/all_gather | solution.py:40
  218.4 34.1 %all-gather.9.cloned.1.call-done = bf16[4,256,2048]{2,1,0:T(8,128)(2,1)} async-done(((bf16[4,256,512]{2,1,0:T(8,128)(2,1)}), bf16[4,256,2048]{2,1,0:T(8,128)(2,1)}) %all-gather.9.cloned.1.call-update) | async-done | bytes 4194320 | tf_op jit(solution)/shard_map/all_gather | solution.py:42
  252.5 0.0 copy-start.2
  252.5 4.2 %fusion = f32[2,256,512]{2,1,0:T(8,128)S(1)} fusion(bf16[4,256,2048]{2,1,0:T(8,128)(2,1)} %all-gather.9.cloned.1.call-done, bf16[3,2048,512]{2,1,0:T(8,128)(2,1)} %all-gather.11.cloned.1.call-done), kind=kOutput, calls=%fused_computation | convolution fusion | flops 1073741824 | bytes 9437184 | tf_op jit(solution)/shard_map/srl,slc->src/dot_general | solution.py:23
  256.7 0.0 copy-done.2
  256.7 3.8 %fusion.4 = f32[2,256,512]{2,1,0:T(8,128)} fusion(f32[2,256,512]{2,1,0:T(8,128)S(1)} %fusion, bf16[4,256,2048]{2,1,0:T(8,128)(2,1)S(1)} %copy-done.2, bf16[3,2048,512]{2,1,0:T(8,128)(2,1)} %all-gather.11.cloned.1.call-done, pred[256,512]{1,0:T(8,128)(4,1)S(1)} %bitcast.52), kind=kOutput, calls=%fused_computation.5 | convolution fusion | flops 1074266112 | bytes 8519680 | tf_op jit(solution)/shard_map/srl,lc->src/dot_general | solution.py:20
  (6 shorter events, 0.1 us)
Async XLA Ops:
  6.5 5.4 %copy-start.4 = (s32[2,4]{1,0:T(2,128)S(1)}, s32[2,4]{1,0:T(2,128)}, u32[]{:S(2)}) copy-start(s32[2,4]{1,0:T(2,128)} %param.12) | copy-start | bytes 100
  6.5 5.9 %copy-start = (bf16[2,256,512]{2,1,0:T(8,128)(2,1)S(1)}, bf16[2,256,512]{2,1,0:T(8,128)(2,1)}, u32[]{:S(2)}) copy-start(bf16[2,256,512]{2,1,0:T(8,128)(2,1)} %param.9) | copy-start | bytes 1572868
  6.5 36.7 %all-gather.5.cloned.1.call-start = ((), (), s32[]{:S(2)}) async-start(), calls=%async_computation | async-start | bytes 3932160 | tf_op jit(solution)/shard_map/all_gather | solution.py:38
  11.9 107.0 %all-gather.7.cloned.1.call-start = ((), (), s32[]{:S(2)}) async-start(), calls=%async_computation.1 | async-start | bytes 4718592 | tf_op jit(solution)/shard_map/all_gather | solution.py:36
  13.3 205.1 %all-gather.11.cloned.1.call-start = ((), (), s32[]{:S(2)}) async-start(), calls=%async_computation.3 | async-start | bytes 7077888 | tf_op jit(solution)/shard_map/all_gather | solution.py:40
  14.0 238.5 %all-gather.9.cloned.1.call-start = ((), (), s32[]{:S(2)}) async-start(), calls=%async_computation.2 | async-start | bytes 5242880 | tf_op jit(solution)/shard_map/all_gather | solution.py:42
  43.3 79.5 %copy-start.3 = (bf16[3,256,2048]{2,1,0:T(8,128)(2,1)S(1)}, bf16[3,256,2048]{2,1,0:T(8,128)(2,1)}, u32[]{:S(2)}) copy-start(bf16[3,256,2048]{2,1,0:T(8,128)(2,1)} %all-gather.5.cloned.1.call-done) | copy-start | bytes 9437188
  118.9 3.9 %copy-start.1 = (bf16[2,2048,512]{2,1,0:T(8,128)(2,1)S(1)}, bf16[2,2048,512]{2,1,0:T(8,128)(2,1)}, u32[]{:S(2)}) copy-start(bf16[2,2048,512]{2,1,0:T(8,128)(2,1)} %all-gather.7.cloned.1.call-done) | copy-start | bytes 12582916
  122.8 2.4 copy-start.5
  252.5 4.2 %copy-start.2 = (bf16[4,256,2048]{2,1,0:T(8,128)(2,1)S(1)}, bf16[4,256,2048]{2,1,0:T(8,128)(2,1)}, u32[]{:S(2)}) copy-start(bf16[4,256,2048]{2,1,0:T(8,128)(2,1)} %all-gather.9.cloned.1.call-done) | copy-start | bytes 12582916
Sparse Core Ops, SparseCore 0:
  12.0 31.2 all-gather.4
  45.5 73.3 all-gather.6
  121.0 97.2 all-gather.10
  219.8 32.6 all-gather.8
where the time goes:
time: 267 us
  waiting for transfers between devices  232 us (87%)
  matrix products  13.3 us (5%)
  between operations  13.3 us (5%)
  other arithmetic  6.44 us (2%)
    all_gather x1, waiting for transfers between devices, body(): operator_cols = lax.all_gather(operators, 'row', axis=1, tiled=True)  92.7 us
    all_gather x1, waiting for transfers between devices, body(): density_cols = lax.all_gather(filtered, 'row', axis=1, tiled=True)  75.6 us
    all_gather x1, waiting for transfers between devices, body(): lax.all_gather(products, 'col', axis=2, tiled=True)  34.1 us
    all_gather x1, waiting for transfers between devices, body(): lax.all_gather(operators, 'col', axis=2, tiled=True)  29.2 us
  transfers between devices with their start and end apart: 4, of which 4 were waited for; matrix products, arithmetic and copies ran while one was open for 3% of the time, Pallas kernels for 0%

commit v1 on v0

--- a/solution.py
+++ b/solution.py
@@ -4,6 +4,19 @@
 from jax.sharding import PartitionSpec as P
 
 BLOCK = 128
+
+
+def ring_gather(x, axis, dim):
+    ways = lax.axis_size(axis)
+    up = [(d, (d + 1) % ways) for d in range(ways)]
+    down = [(d, (d - 1) % ways) for d in range(ways)]
+    earlier, later = ([x], [x])
+    for _ in range(ways // 2):
+        earlier.append(lax.ppermute(earlier[-1], axis, up))
+    for _ in range((ways - 1) // 2):
+        later.append(lax.ppermute(later[-1], axis, down))
+    line = jnp.concatenate([*earlier[::-1], *later[1:]], axis=dim)
+    return jnp.roll(line, (lax.axis_index(axis) - ways // 2) * x.shape[dim], axis=dim)
 
 
 def widen(keep):
@@ -35,7 +48,7 @@
     operators = jnp.concatenate([kohn_sham, smat[None]], axis=0)
     density_cols = lax.all_gather(filtered, "row", axis=1, tiled=True)
     cols_part = density_cols
-    products = first_terms(lax.all_gather(operators, "col", axis=2, tiled=True), cols_part)
+    products = first_terms(ring_gather(operators, "col", 2), cols_part)
     products = products.astype(jnp.bfloat16)
     operator_cols = lax.all_gather(operators, "row", axis=1, tiled=True)
     cols_part = operator_cols

time: 267 us -> 235 us (0.88)
  waiting for transfers between devices: 232 us -> 186 us
  local copies, waits for them, and re-layouts: 1.63 us -> 7.6 us
  other arithmetic: 6.44 us -> 10.1 us
    all_gather x1, waiting for transfers between devices: 75.6 us -> 33.6 us  [body(): density_cols = lax.all_gather(filtered, 'row', axis=1, tiled=True)]
    all_gather x1 -> x0, waiting for transfers between devices: 29.2 us -> none  [body(): lax.all_gather(operators, 'col', axis=2, tiled=True)]
    ppermute x0 -> x3, waiting for transfers between devices: none -> 27.1 us  [the longest x2 27.1 us: ring_gather(): earlier.append(lax.ppermute(earlier[-1], axis, up))]
    unnamed x15 -> x14, local copies, waits for them, and re-layouts: 0.23 us -> 5.24 us
  transfers between devices with their start and end apart: 4 -> 6, of which waited for: 4 -> 5; matrix products, arithmetic and copies ran while one was open for 3% -> 9% of each run, Pallas kernels for 0% -> 0%
where the time goes in v1:
time: 235 us; the launch traced here: 234 us
  waiting for transfers between devices  186 us (79%)
  matrix products  14.9 us (6%)
  between operations  13.2 us (6%)
  other arithmetic  10.1 us (4%)
  local copies, waits for them, and re-layouts  7.6 us (3%)
    all_gather x1, waiting for transfers between devices, body(): operator_cols = lax.all_gather(operators, 'row', axis=1, tiled=True)  91.1 us
    all_gather x1, waiting for transfers between devices, body(): lax.all_gather(products, 'col', axis=2, tiled=True)  34.3 us
    all_gather x1, waiting for transfers between devices, body(): density_cols = lax.all_gather(filtered, 'row', axis=1, tiled=True)  33.6 us
    ppermute x2, waiting for transfers between devices, ring_gather(): earlier.append(lax.ppermute(earlier[-1], axis, up))  27.1 us
    unnamed x14, local copies, waits for them, and re-layouts  5.24 us
  transfers between devices with their start and end apart: 6, of which 5 were waited for; matrix products, arithmetic and copies ran while one was open for 9% of the time, Pallas kernels for 0%

profile of v1, /device:TPU:0, one launch (start us, length us, event | category | flops | bytes accessed | tf_op | source)
XLA Modules:
  0.0 234.2 jit_solution(5810524558689671142)
XLA Ops:
  6.5 0.0 all-gather.4.cloned.1.call-start
  6.5 0.7 broadcast_compare_fusion
  7.2 0.3 broadcast_in_dim.68
  7.6 0.1 copy.22
  7.7 1.9 broadcast_select_fusion
  9.5 0.0 all-gather.4.cloned.1.call-update
  9.6 0.0 all-gather.8.cloned.1.call-start
  9.6 0.7 broadcast_compare_fusion.2
  10.3 0.3 broadcast_in_dim.61
  10.7 0.1 copy.23
  10.7 0.7 broadcast_compare_fusion.1
  11.4 0.3 broadcast_in_dim.64
  11.8 1.0 fusion.11
  12.8 1.1 broadcast_select_fusion.1
  13.9 1.0 pad_maximum_fusion.1
  14.9 0.0 all-gather.8.cloned.1.call-update
  14.9 0.0 all-gather.6.cloned.1.call-start
  15.0 0.5 collective-permute-start
  15.5 11.8 %collective-permute-done = bf16[3,256,512]{2,1,0:T(8,128)(2,1)S(1)} collective-permute-done((bf16[3,256,512]{2,1,0:T(8,128)(2,1)}, bf16[3,256,512]{2,1,0:T(8,128)(2,1)S(1)}, u32[]{:S(2)}, u32[]{:S(2)}) %collective-permute-start) | collective-permute-done | bytes 786464 | tf_op jit(solution)/shard_map/ppermute | solution.py:15
  27.3 0.0 collective-permute-start.1
  27.4 1.7 collective-permute-start.2
  29.1 15.2 %collective-permute-done.1 = bf16[3,256,512]{2,1,0:T(8,128)(2,1)S(1)} collective-permute-done((bf16[3,256,512]{2,1,0:T(8,128)(2,1)S(1)}, bf16[3,256,512]{2,1,0:T(8,128)(2,1)S(1)}, u32[]{:S(2)}, u32[]{:S(2)}) %collective-permute-start.1) | collective-permute-done | bytes 786464 | tf_op jit(solution)/shard_map/ppermute | solution.py:15
  44.3 1.0 constant_dynamic-update-slice_fusion.7
  45.3 1.0 constant_dynamic-update-slice_fusion.6
  46.3 1.0 constant_dynamic-update-slice_fusion.5
  47.3 0.0 collective-permute-done.2
  47.3 1.0 constant_dynamic-update-slice_fusion.4
  48.3 1.0 constant_dynamic-update-slice_fusion.3
  49.3 1.0 constant_dynamic-update-slice_fusion.2
  50.3 1.0 constant_dynamic-update-slice_fusion.1
  51.3 0.9 constant_dynamic-update-slice_fusion
  52.2 33.6 %all-gather.4.cloned.1.call-done = bf16[2,2048,512]{2,1,0:T(8,128)(2,1)} async-done(((bf16[2,256,512]{2,1,0:T(8,128)(2,1)}), bf16[2,2048,512]{2,1,0:T(8,128)(2,1)}) %all-gather.4.cloned.1.call-update) | async-done | bytes 4194320 | tf_op jit(solution)/shard_map/all_gather | solution.py:49
  85.8 0.0 copy-start
  85.8 3.9 %fusion.10 = bf16[2,256,512]{2,1,0:T(8,128)(2,1)S(1)} fusion(bf16[2,2048,512]{2,1,0:T(8,128)(2,1)} %all-gather.4.cloned.1.call-done, bf16[3,256,4096]{2,1,0:T(8,128)(2,1)} %constant_dynamic-update-slice_fusion, s32[]{:T(128)S(6)} %add.13, s32[]{:T(128)S(6)} %select_n.31), kind=kOutput, calls=%fused_computation.10 | convolution fusion | flops 1074003968 | bytes 5767176 | tf_op jit(solution)/shard_map/rl,slc->src/dot_general | solution.py:28
  89.7 0.0 copy-done
  89.7 0.0 copy-start.2
  89.7 2.9 %fusion.7 = bf16[2,256,512]{2,1,0:T(8,128)(2,1)S(1)} fusion(bf16[2,2048,512]{2,1,0:T(8,128)(2,1)S(1)} %copy-done, bf16[3,256,4096]{2,1,0:T(8,128)(2,1)} %constant_dynamic-update-slice_fusion, s32[]{:T(128)S(6)} %select_n.31), kind=kOutput, calls=%fused_computation.8 | convolution fusion | flops 1074003968 | bytes 7864324 | tf_op jit(solution)/shard_map/srl,slc->src/dot_general | solution.py:27
  92.6 1.1 pad_maximum_fusion
  93.7 0.0 all-gather.6.cloned.1.call-update
  93.7 0.0 copy-done.2
  93.8 0.3 broadcast_in_dim.58
  94.1 0.1 copy.24
  94.2 91.1 %all-gather.8.cloned.1.call-done = bf16[3,2048,512]{2,1,0:T(8,128)(2,1)} async-done(((bf16[3,256,512]{2,1,0:T(8,128)(2,1)}), bf16[3,2048,512]{2,1,0:T(8,128)(2,1)}) %all-gather.8.cloned.1.call-update) | async-done | bytes 6291472 | tf_op jit(solution)/shard_map/all_gather | solution.py:53
  185.3 34.3 %all-gather.6.cloned.1.call-done = bf16[4,256,2048]{2,1,0:T(8,128)(2,1)} async-done(((bf16[4,256,512]{2,1,0:T(8,128)(2,1)}), bf16[4,256,2048]{2,1,0:T(8,128)(2,1)}) %all-gather.6.cloned.1.call-update) | async-done | bytes 4194320 | tf_op jit(solution)/shard_map/all_gather | solution.py:55
  219.6 0.0 copy-start.1
  219.6 4.2 %fusion = f32[2,256,512]{2,1,0:T(8,128)S(1)} fusion(bf16[4,256,2048]{2,1,0:T(8,128)(2,1)} %all-gather.6.cloned.1.call-done, bf16[3,2048,512]{2,1,0:T(8,128)(2,1)} %all-gather.8.cloned.1.call-done), kind=kOutput, calls=%fused_computation | convolution fusion | flops 1073741824 | bytes 9437184 | tf_op jit(solution)/shard_map/srl,slc->src/dot_general | solution.py:36
  223.8 0.0 copy-done.1
  223.8 3.8 %fusion.6 = f32[2,256,512]{2,1,0:T(8,128)} fusion(f32[2,256,512]{2,1,0:T(8,128)S(1)} %fusion, bf16[4,256,2048]{2,1,0:T(8,128)(2,1)S(1)} %copy-done.1, bf16[3,2048,512]{2,1,0:T(8,128)(2,1)} %all-gather.8.cloned.1.call-done, pred[256,512]{1,0:T(8,128)(4,1)S(1)} %bitcast.51), kind=kOutput, calls=%fused_computation.7 | convolution fusion | flops 1074266112 | bytes 8519680 | tf_op jit(solution)/shard_map/srl,lc->src/dot_general | solution.py:33
  (5 shorter events, 0.1 us)
Async XLA Ops:
  6.5 79.3 %all-gather.4.cloned.1.call-start = ((), (), s32[]{:S(2)}) async-start(), calls=%async_computation | async-start | bytes 4718592 | tf_op jit(solution)/shard_map/all_gather | solution.py:49
  9.6 175.7 %all-gather.8.cloned.1.call-start = ((), (), s32[]{:S(2)}) async-start(), calls=%async_computation.2 | async-start | bytes 7077888 | tf_op jit(solution)/shard_map/all_gather | solution.py:53
  14.9 204.7 %all-gather.6.cloned.1.call-start = ((), (), s32[]{:S(2)}) async-start(), calls=%async_computation.1 | async-start | bytes 5242880 | tf_op jit(solution)/shard_map/all_gather | solution.py:55
  15.0 12.3 %collective-permute-start = (bf16[3,256,512]{2,1,0:T(8,128)(2,1)}, bf16[3,256,512]{2,1,0:T(8,128)(2,1)S(1)}, u32[]{:S(2)}, u32[]{:S(2)}) collective-permute-start(bf16[3,256,512]{2,1,0:T(8,128)(2,1)} %pad_maximum_fusion.1), channel_id=1, source_target_pairs={{0,1},{1,2},{2,3},{3,0},{4,5},{5,6},{6,7},{7,4},{8,9},{9,10},{10,1... | collective-permute-start | bytes 2359304 | tf_op jit(solution)/shard_map/ppermute | solution.py:15
  27.3 17.0 %collective-permute-start.1 = (bf16[3,256,512]{2,1,0:T(8,128)(2,1)S(1)}, bf16[3,256,512]{2,1,0:T(8,128)(2,1)S(1)}, u32[]{:S(2)}, u32[]{:S(2)}) collective-permute-start(bf16[3,256,512]{2,1,0:T(8,128)(2,1)S(1)} %collective-permute-done), channel_id=1, source_target_pairs={{0,1},{1,2},{2,3},{3,0},{4,5},{5,6},{6,7},{7,4},{8,9},{9,10},{10,1... | collective-permute-start | bytes 2359304 | tf_op jit(solution)/shard_map/ppermute | solution.py:15
  27.4 20.0 %collective-permute-start.2 = (bf16[3,256,512]{2,1,0:T(8,128)(2,1)}, bf16[3,256,512]{2,1,0:T(8,128)(2,1)S(1)}, u32[]{:S(2)}, u32[]{:S(2)}) collective-permute-start(bf16[3,256,512]{2,1,0:T(8,128)(2,1)} %pad_maximum_fusion.1), channel_id=1, source_target_pairs={{0,3},{1,0},{2,1},{3,2},{4,7},{5,4},{6,5},{7,6},{8,11},{9,8},{10,9... | collective-permute-start | bytes 2359304 | tf_op jit(solution)/shard_map/ppermute | solution.py:17
  85.8 3.9 %copy-start = (bf16[2,2048,512]{2,1,0:T(8,128)(2,1)S(1)}, bf16[2,2048,512]{2,1,0:T(8,128)(2,1)}, u32[]{:S(2)}) copy-start(bf16[2,2048,512]{2,1,0:T(8,128)(2,1)} %all-gather.4.cloned.1.call-done) | copy-start | bytes 12582916
  89.7 4.0 %copy-start.2 = (s32[2,4]{1,0:T(2,128)S(1)}, s32[2,4]{1,0:T(2,128)}, u32[]{:S(2)}) copy-start(s32[2,4]{1,0:T(2,128)} %param.13) | copy-start | bytes 100
  219.6 4.2 %copy-start.1 = (bf16[4,256,2048]{2,1,0:T(8,128)(2,1)S(1)}, bf16[4,256,2048]{2,1,0:T(8,128)(2,1)}, u32[]{:S(2)}) copy-start(bf16[4,256,2048]{2,1,0:T(8,128)(2,1)} %all-gather.6.cloned.1.call-done) | copy-start | bytes 12582916
Sparse Core Ops, SparseCore 0:
  9.7 76.0 all-gather.3
  88.0 97.2 all-gather.7
  186.9 32.6 all-gather.5
